TPU v7x, 256 devices: a whole 4x4x8 slice. The times are simulated.
256 devices in a mesh: row: 8 (over z), col: 32 (over y, x, core).
Axes of the slice: x: 4, y: 4, z: 8, core: 2. Of those that a mesh axis runs over, the one named last changes fastest.
Arguments:
- ancestor_inverse: bfloat16 [24576, 24576], P('row', 'col'), may hold values from -6 to 6
- factor_slots: bfloat16 [3, 16384, 512], P(None, ('row', 'col')), may hold values from -0.25 to 0.25
- slot_tiles: int32 [3, 64], replicated, may hold values from -1 to 95, as said below
- parent_factor: bfloat16 [2, 512, 512], replicated, may hold values from -0.25 to 0.25
- diag_inverse: float32 [3, 512, 512], replicated, may hold values from -6 to 6
Outputs:
- inverse_panels: bfloat16 [3, 24576, 512], P(None, ('row', 'col'))
- diag_blocks: float32 [3, 512, 512], replicated
- parent_blocks: float32 [2, 512, 512], replicated
Inputs may be any that keep to these rules, and one draw needn't show every extreme that they name: `slot_tiles`: entries b * 2 to b * 2 + 1 of a supernode's row are the slots of column block b: each is -1 (empty) or names a tile from b * 3 to b * 3 + 2, no tile twice; in each supernode some block has all its slots filled. `factor_slots`: rows of an empty slot are not part of the factor.
All inputs are finite; a program needn't handle non-finite values.
Results may differ from a plain program's by a relative error of at most 0.00075.
Values may be sent and summed in bfloat16 or wider, within the bound.
No kernel may reach another device: no remote copies, remote signals or barrier semaphores. Data moves between devices by JAX's collectives and lax.ppermute only.
A program may use at most 128 MiB of HBM per device.

v0:
```python
import jax
import jax.numpy as jnp
from jax import lax
from jax.sharding import PartitionSpec as P

TILE = 256
CAP = 2
exact_mode = lax.Precision.HIGHEST


def spread(shard, axis, root):
    mine = lax.axis_index(axis) == root
    return lax.psum(jnp.where(mine, shard, jnp.zeros_like(shard)), axis)


def padded_block(slot_data, slot_ids, block_index, tiles_per_block, tile_rows):
    local_tile = slot_ids - block_index * tiles_per_block
    pieces = []
    for tile_index in range(tiles_per_block):
        chosen = jnp.zeros((tile_rows, slot_data.shape[1]), slot_data.dtype)
        for member in range(slot_ids.shape[0]):
            chosen = jnp.where(
                local_tile[member] == tile_index,
                slot_data[member * tile_rows : (member + 1) * tile_rows],
                chosen,
            )
        pieces.append(chosen)
    return jnp.concatenate(pieces, axis=0)


def chosen_columns(inverse_block, slot_ids, block_index, tiles_per_block, tile_rows):
    local_tile = jnp.clip(slot_ids - block_index * tiles_per_block, 0, tiles_per_block - 1)
    pieces = [
        lax.dynamic_slice_in_dim(inverse_block, local_tile[member] * tile_rows, tile_rows, 1)
        for member in range(slot_ids.shape[0])
    ]
    return jnp.concatenate(pieces, axis=1)


def masked_rows(slot_data, slot_ids, tile_rows):
    live_rows = jnp.repeat(slot_ids >= 0, tile_rows)
    return jnp.where(live_rows[:, None], slot_data, jnp.zeros_like(slot_data))


def on_device(ancestor_inverse, factor_slots, slot_tiles, parent_factor, diag_inverse):
    row_count = lax.axis_size("row")
    col_count = lax.axis_size("col")
    row_index = lax.axis_index("row")
    col_index = lax.axis_index("col")
    block_rows, block_cols = ancestor_inverse.shape
    tile_rows = TILE
    tiles_per_block = block_cols // tile_rows
    node_count = factor_slots.shape[0]
    slot_count = CAP
    slot_rows = slot_count * tile_rows
    groups_per_row = col_count // row_count
    panel_rows = block_rows // col_count
    own_block = row_index * groups_per_row + col_index // row_count
    own_offset = col_index % row_count * panel_rows
    slot_start = col_index % groups_per_row * slot_rows
    owner_row = col_index // groups_per_row

    def finish(node, first_total, second_total, prev_diag):
        if node == 0:
            return (diag_inverse[0] - first_total, None)
        parent_link = parent_factor[node - 1].astype(jnp.float32)
        upper = -(second_total + jnp.dot(prev_diag, parent_link, precision=exact_mode))
        diagonal = (
            diag_inverse[node] - first_total - jnp.dot(parent_link.T, upper, precision=exact_mode)
        )
        return (diagonal, upper)

    def node_sums(node, first_part, second_part):
        if node == 0:
            return (lax.psum(first_part, ("row", "col")), None)
        return lax.psum((first_part, second_part), ("row", "col"))

    panels = []
    diagonals = []
    parents = []
    previous = None
    prev_diag = None
    for node in range(node_count):
        row_slots = lax.all_gather(factor_slots[node], "col", axis=0, tiled=True)
        mine = lax.dynamic_slice_in_dim(row_slots, slot_start, slot_rows, 0)
        col_slots = spread(mine, "row", owner_row)
        tiles_node = slot_tiles[node]
        col_ids = lax.dynamic_slice_in_dim(tiles_node, col_index * slot_count, slot_count)
        prepare_columns = chosen_columns(
            ancestor_inverse, col_ids, col_index, tiles_per_block, tile_rows
        )
        prepare_weights = masked_rows(col_slots, col_ids, tile_rows)
        own_ids = lax.dynamic_slice_in_dim(tiles_node, own_block * slot_count, slot_count)
        own_slots = lax.dynamic_slice_in_dim(
            row_slots, col_index // row_count * slot_rows, slot_rows, 0
        )
        own_padded = padded_block(own_slots, own_ids, own_block, tiles_per_block, tile_rows)
        own_rows = lax.dynamic_slice_in_dim(own_padded, own_offset, panel_rows, 0)
        row_padded = None
        columns, weights, own_rows, row_padded = (
            prepare_columns,
            prepare_weights,
            own_rows.astype(jnp.float32),
            row_padded,
        )
        second_part = None
        if node > 0:
            second_part = jnp.dot(previous.T, own_rows, precision=exact_mode)
        summed = lax.psum_scatter(
            jnp.dot(columns, weights, preferred_element_type=jnp.float32),
            "col",
            scatter_dimension=0,
            tiled=True,
        )
        column = -summed
        if node > 0:
            advance_parent_link = parent_factor[node - 1].astype(jnp.float32)
            column = column - jnp.dot(previous, advance_parent_link, precision=exact_mode)
        first_part = jnp.dot(own_rows.T, column, precision=exact_mode)
        first_total, second_total = node_sums(node, first_part, second_part)
        diagonal, upper = finish(node, first_total, second_total, prev_diag)
        panels.append(column.astype(jnp.bfloat16))
        diagonals.append(diagonal)
        if node > 0:
            parents.append(upper)
        previous = column
        prev_diag = diagonal
    return (jnp.stack(panels), jnp.stack(diagonals), jnp.stack(parents))


def solution(mesh):
    placed = (P("row", "col"), P(None, ("row", "col"), None), P(), P(), P())
    return jax.shard_map(
        on_device,
        mesh=mesh,
        in_specs=placed,
        out_specs=(P(None, ("row", "col"), None), P(), P()),
        check_vma=False,
    )
```

profile of v0, /device:TPU:8, one launch (start us, length us, event | category | flops | bytes accessed | tf_op | source)
XLA Modules:
  0.0 841.9 jit_solution(13287973406344088835)
XLA Ops:
  7.2 1.6 fusion.71
  10.4 51.9 %all-gather.9.cloned.1.call-done = bf16[1,2048,512]{2,1,0:T(8,128)(2,1)} async-done(((bf16[1,64,512]{2,1,0:T(8,128)(2,1)}), bf16[1,2048,512]{2,1,0:T(8,128)(2,1)}) %all-gather.9.cloned.1.call-update) | async-done | bytes 2097168 | tf_op jit(solution)/shard_map/all_gather | solution.py:84
  62.3 1.9 select_bitcast_fusion.1
  64.2 49.2 %all-gather.7.cloned.1.call-done = bf16[1,2048,512]{2,1,0:T(8,128)(2,1)} async-done(((bf16[1,64,512]{2,1,0:T(8,128)(2,1)}), bf16[1,2048,512]{2,1,0:T(8,128)(2,1)}) %all-gather.7.cloned.1.call-update) | async-done | bytes 2097168 | tf_op jit(solution)/shard_map/all_gather | solution.py:84
  113.4 1.9 select_bitcast_fusion.2
  115.3 49.2 %all-gather.11.cloned.1.call-done = bf16[1,2048,512]{2,1,0:T(8,128)(2,1)} async-done(((bf16[1,64,512]{2,1,0:T(8,128)(2,1)}), bf16[1,2048,512]{2,1,0:T(8,128)(2,1)}) %all-gather.11.cloned.1.call-update) | async-done | bytes 2097168 | tf_op jit(solution)/shard_map/all_gather | solution.py:84
  164.5 1.9 select_bitcast_fusion
  172.6 6.8 constant_dynamic-slice_fusion.4
  179.5 66.0 %all-reduce.7.cloned.1.call-done = (bf16[512,512]{1,0:T(8,128)(2,1)}, bf16[512,512]{1,0:T(8,128)(2,1)}, bf16[512,512]{1,0:T(8,128)(2,1)}) async-done(((bf16[512,512]{1,0:T(8,128)(2,1)}, bf16[512,512]{1,0:T(8,128)(2,1)}, bf16[512,512]{1,0:T(8,128)(2,1)}), (bf16[512,512]{1,0:T(8,128)(2,1)}, bf16[512,512]{1,0:T(8,128)(2,1)}, bf16[512,512]{1,0:T(8,128)(2,1)})) %all-reduce.7.cloned.1.call-update) | async-done | bytes 1572880 | tf_op jit(solution)/shard_map/psum | solution.py:13
  245.4 6.5 fusion.4
  252.2 6.5 fusion
  258.8 5.5 fusion.8
  277.3 1.2 select_bitcast_fusion.8
  278.5 2.0 select_bitcast_fusion.10
  280.5 1.2 select_bitcast_fusion.5
  281.7 63.3 %reduce-scatter.6.cloned.1.call-done = f32[96,512]{1,0:T(8,128)} async-done(((f32[3072,512]{1,0:T(8,128)}), f32[96,512]{1,0:T(8,128)}) %reduce-scatter.6.cloned.1.call-update) | async-done | bytes 196624 | tf_op jit(solution)/shard_map/reduce_scatter | solution.py:109
  345.0 97.1 %reduce-scatter.4.cloned.1.call-done = f32[96,512]{1,0:T(8,128)} async-done(((f32[3072,512]{1,0:T(8,128)}), f32[96,512]{1,0:T(8,128)}) %reduce-scatter.4.cloned.1.call-update) | async-done | bytes 196624 | tf_op jit(solution)/shard_map/reduce_scatter | solution.py:109
  442.1 1.4 convolution_subtract_fusion.1
  443.5 1.7 fusion.69
  445.2 94.2 %reduce-scatter.8.cloned.1.call-done = f32[96,512]{1,0:T(8,128)} async-done(((f32[3072,512]{1,0:T(8,128)}), f32[96,512]{1,0:T(8,128)}) %reduce-scatter.8.cloned.1.call-update) | async-done | bytes 196624 | tf_op jit(solution)/shard_map/reduce_scatter | solution.py:109
  539.4 1.3 convolution_subtract_fusion
  540.7 1.7 fusion.67
  542.5 1.7 fusion.64
  544.2 1.7 fusion.39
  545.8 1.8 fusion.41
  548.5 274.5 %all-reduce.5.cloned.1.call-done = (f32[512,512]{1,0:T(8,128)}, f32[512,512]{1,0:T(8,128)}, f32[512,512]{1,0:T(8,128)}, f32[512,512]{1,0:T(8,128)}, f32[512,512]{1,0:T(8,128)}) async-done(((f32[512,512]{1,0:T(8,128)}, f32[512,512]{1,0:T(8,128)}, f32[512,512]{1,0:T(8,128)}, f32[512,512]{1,0:T(8,128)}, f32[512,512]{1,0:T(8,128)}), (f32[512,512]{1,0:T(8,128)}, f32[512,512]{1,0:T(8,128)}, f32[512,512]{1,0:T(8,128)}, ...) | async-done | bytes 5242896 | tf_op jit(solution)/shard_map/psum | solution.py:76
  823.1 1.9 fusion.29
  825.6 2.6 fusion.13
  828.2 1.1 fusion.16
  830.4 1.1 fusion.15
  831.5 1.5 pad_maximum_fusion.1
  833.0 2.0 pad_maximum_fusion
  (55 shorter events, 8.1 us)
Async XLA Ops:
  7.2 159.4 %copy-start.8 = (s32[3,64]{1,0:T(4,128)S(1)}, s32[3,64]{1,0:T(4,128)}, u32[]{:S(2)}) copy-start(s32[3,64]{1,0:T(4,128)} %param.7) | copy-start | bytes 2308
  7.2 55.1 %all-gather.9.cloned.1.call-start = ((), (), s32[]{:S(2)}) async-start(), calls=%async_computation.7 | async-start | bytes 2162688 | tf_op jit(solution)/shard_map/all_gather | solution.py:84
  8.8 104.6 %all-gather.7.cloned.1.call-start = ((), (), s32[]{:S(2)}) async-start(), calls=%async_computation.6 | async-start | bytes 2162688 | tf_op jit(solution)/shard_map/all_gather | solution.py:84
  9.6 154.9 %all-gather.11.cloned.1.call-start = ((), (), s32[]{:S(2)}) async-start(), calls=%async_computation.8 | async-start | bytes 2162688 | tf_op jit(solution)/shard_map/all_gather | solution.py:84
  10.3 235.1 %all-reduce.7.cloned.1.call-start = ((), (), s32[]{:S(2)}) async-start(), calls=%async_computation.10 | async-start | bytes 3145728 | tf_op jit(solution)/shard_map/psum | solution.py:13
  166.5 178.5 %reduce-scatter.6.cloned.1.call-start = ((), (), s32[]{:S(2)}) async-start(), calls=%async_computation.4 | async-start | bytes 6488064 | tf_op jit(solution)/shard_map/reduce_scatter | solution.py:109
  252.0 190.1 %reduce-scatter.4.cloned.1.call-start = ((), (), s32[]{:S(2)}) async-start(), calls=%async_computation.3 | async-start | bytes 6488064 | tf_op jit(solution)/shard_map/reduce_scatter | solution.py:109
  258.7 280.7 %reduce-scatter.8.cloned.1.call-start = ((), (), s32[]{:S(2)}) async-start(), calls=%async_computation.5 | async-start | bytes 6488064 | tf_op jit(solution)/shard_map/reduce_scatter | solution.py:109
  264.4 177.7 %copy-start = (bf16[2,512,512]{2,1,0:T(8,128)(2,1)S(1)}, bf16[2,512,512]{2,1,0:T(8,128)(2,1)}, u32[]{:S(2)}) copy-start(bf16[2,512,512]{2,1,0:T(8,128)(2,1)} %param.8) | copy-start | bytes 3145732
  264.4 558.7 %all-reduce.5.cloned.1.call-start = ((), (), s32[]{:S(2)}) async-start(), calls=%async_computation.9 | async-start | bytes 10485760 | tf_op jit(solution)/shard_map/psum | solution.py:76
  443.5 100.7 %copy-start.2 = (f32[96,512]{1,0:T(8,128)S(1)}, f32[96,512]{1,0:T(8,128)}, u32[]{:S(2)}) copy-start(f32[96,512]{1,0:T(8,128)} %reduce-scatter.4.cloned.1.call-done) | copy-start | bytes 589828
  540.7 5.1 copy-start.4
  540.7 5.1 copy-start.5
  823.0 2.5 copy-start.1
  825.0 3.2 copy-start.7
  828.2 1.2 copy-start.3
  828.2 2.2 copy-start.6
Sparse Core Ops, SparseCore 0:
  11.1 51.0 all-gather.8
  65.4 47.9 all-gather.6
  116.5 47.9 all-gather.10
  167.0 78.4 all-reduce.6
  252.1 92.8 reduce-scatter.5
  348.9 93.1 reduce-scatter.3
  446.1 93.2 reduce-scatter.7
  547.8 275.1 all-reduce.4
where the time goes:
time: 843 us; the launch traced here: 842 us
  waiting for transfers between devices  747 us (89%)
  matrix products  35.6 us (4%)
  between operations  29.7 us (4%)
  other arithmetic  16.8 us (2%)
  local copies, waits for them, and re-layouts  12.5 us (1%)
    psum x1, waiting for transfers between devices, node_sums(): return lax.psum((first_part, second_part), ('row', 'col'))  275 us
    reduce_scatter x3, waiting for transfers between devices, on_device(): lax.psum_scatter(jnp.dot(columns, weights, preferred_element_type=jnp.flo...  255 us
    all_gather x3, waiting for transfers between devices, on_device(): row_slots = lax.all_gather(factor_slots[node], 'col', axis=0, tiled=True)  150 us
    psum x1, waiting for transfers between devices, spread(): return lax.psum(jnp.where(mine, shard, jnp.zeros_like(shard)), axis)  66 us
    dot_general x3, matrix products, on_device(): jnp.dot(columns, weights, preferred_element_type=jnp.float32)  18.5 us
  transfers between devices with their start and end apart: 8, of which 8 were waited for; matrix products, arithmetic and copies ran while one was open for 4% of the time, Pallas kernels for 0%

commit v1 on v0

--- a/solution.py
+++ b/solution.py
@@ -10,7 +10,7 @@
 
 def spread(shard, axis, root):
     mine = lax.axis_index(axis) == root
-    return lax.psum(jnp.where(mine, shard, jnp.zeros_like(shard)), axis)
+    return jnp.sum(lax.all_gather(jnp.where(mine, shard, jnp.zeros_like(shard)), axis), axis=0)
 
 
 def padded_block(slot_data, slot_ids, block_index, tiles_per_block, tile_rows):

time: 843 us -> 925 us (1.097)
  waiting for transfers between devices: 747 us -> 818 us
  other arithmetic: 16.8 us -> 28 us
    all_gather x0 -> x3, waiting for transfers between devices: none -> 131 us  [spread(): lax.all_gather(jnp.where(mine, shard, jnp.zeros_like(shard)), axis)]
    psum x1 -> x0, waiting for transfers between devices: 66 us -> none  [spread(): return lax.psum(jnp.where(mine, shard, jnp.zeros_like(shard)), axis)]
    reduce_sum x0 -> x3, other arithmetic: none -> 11.2 us  [spread(): jnp.sum(lax.all_gather(jnp.where(mine, shard, jnp.zeros_like(shard)), axi...]
  transfers between devices with their start and end apart: 8 -> 10, of which waited for: 8 -> 10; matrix products, arithmetic and copies ran while one was open for 4% -> 6% of each run, Pallas kernels for 0% -> 0%
where the time goes in v1:
time: 925 us; the launch traced here: 924 us
  waiting for transfers between devices  818 us (88%)
  matrix products  35.6 us (4%)
  between operations  29.6 us (3%)
  other arithmetic  28 us (3%)
  local copies, waits for them, and re-layouts  12.4 us (1%)
    psum x1, waiting for transfers between devices, node_sums(): return lax.psum((first_part, second_part), ('row', 'col'))  274 us
    reduce_scatter x3, waiting for transfers between devices, on_device(): lax.psum_scatter(jnp.dot(columns, weights, preferred_element_type=jnp.flo...  261 us
    all_gather x3, waiting for transfers between devices, on_device(): row_slots = lax.all_gather(factor_slots[node], 'col', axis=0, tiled=True)  150 us
    all_gather x3, waiting for transfers between devices, spread(): lax.all_gather(jnp.where(mine, shard, jnp.zeros_like(shard)), axis)  131 us
  transfers between devices with their start and end apart: 10, of which 10 were waited for; matrix products, arithmetic and copies ran while one was open for 6% of the time, Pallas kernels for 0%

profile of v1, /device:TPU:8, one launch (start us, length us, event | category | flops | bytes accessed | tf_op | source)
XLA Modules:
  0.0 923.9 jit_solution(16023581032821552080)
XLA Ops:
  7.2 1.6 fusion.71
  10.4 51.9 %all-gather.16.cloned.1.call-done = bf16[1,2048,512]{2,1,0:T(8,128)(2,1)} async-done(((bf16[1,64,512]{2,1,0:T(8,128)(2,1)}), bf16[1,2048,512]{2,1,0:T(8,128)(2,1)}) %all-gather.16.cloned.1.call-update) | async-done | bytes 2097168 | tf_op jit(solution)/shard_map/all_gather | solution.py:84
  62.3 1.9 dynamic-slice_select_fusion.2
  64.3 49.1 %all-gather.18.cloned.1.call-done = bf16[1,2048,512]{2,1,0:T(8,128)(2,1)} async-done(((bf16[1,64,512]{2,1,0:T(8,128)(2,1)}), bf16[1,2048,512]{2,1,0:T(8,128)(2,1)}) %all-gather.18.cloned.1.call-update) | async-done | bytes 2097168 | tf_op jit(solution)/shard_map/all_gather | solution.py:84
  113.4 1.9 dynamic-slice_select_fusion.1
  115.4 49.1 %all-gather.20.cloned.1.call-done = bf16[1,2048,512]{2,1,0:T(8,128)(2,1)} async-done(((bf16[1,64,512]{2,1,0:T(8,128)(2,1)}), bf16[1,2048,512]{2,1,0:T(8,128)(2,1)}) %all-gather.20.cloned.1.call-update) | async-done | bytes 2097168 | tf_op jit(solution)/shard_map/all_gather | solution.py:84
  164.5 1.9 dynamic-slice_select_fusion
  172.5 6.8 constant_dynamic-slice_fusion.4
  179.3 41.4 %all-gather.22.cloned.1.call-done = bf16[1,4096,512]{2,1,0:T(8,128)(2,1)} async-done(((bf16[1,512,512]{2,1,0:T(8,128)(2,1)}), bf16[1,4096,512]{2,1,0:T(8,128)(2,1)}) %all-gather.22.cloned.1.call-update) | async-done | bytes 4194320 | tf_op jit(solution)/shard_map/all_gather | solution.py:13
  220.7 3.8 reduce_sum.36
  224.5 6.5 fusion
  231.2 44.5 %all-gather.24.cloned.1.call-done = bf16[1,4096,512]{2,1,0:T(8,128)(2,1)} async-done(((bf16[1,512,512]{2,1,0:T(8,128)(2,1)}), bf16[1,4096,512]{2,1,0:T(8,128)(2,1)}) %all-gather.24.cloned.1.call-update) | async-done | bytes 4194320 | tf_op jit(solution)/shard_map/all_gather | solution.py:13
  275.7 3.7 reduce_sum.37
  279.4 6.5 fusion.4
  286.1 44.6 %all-gather.26.cloned.1.call-done = bf16[1,4096,512]{2,1,0:T(8,128)(2,1)} async-done(((bf16[1,512,512]{2,1,0:T(8,128)(2,1)}), bf16[1,4096,512]{2,1,0:T(8,128)(2,1)}) %all-gather.26.cloned.1.call-update) | async-done | bytes 4194320 | tf_op jit(solution)/shard_map/all_gather | solution.py:13
  330.7 3.7 reduce_sum.38
  334.5 5.5 fusion.8
  355.3 2.0 select_bitcast_fusion.7
  357.3 69.7 %reduce-scatter.4.cloned.1.call-done = f32[96,512]{1,0:T(8,128)} async-done(((f32[3072,512]{1,0:T(8,128)}), f32[96,512]{1,0:T(8,128)}) %reduce-scatter.4.cloned.1.call-update) | async-done | bytes 196624 | tf_op jit(solution)/shard_map/reduce_scatter | solution.py:109
  427.0 97.3 %reduce-scatter.6.cloned.1.call-done = f32[96,512]{1,0:T(8,128)} async-done(((f32[3072,512]{1,0:T(8,128)}), f32[96,512]{1,0:T(8,128)}) %reduce-scatter.6.cloned.1.call-update) | async-done | bytes 196624 | tf_op jit(solution)/shard_map/reduce_scatter | solution.py:109
  524.2 1.4 convolution_subtract_fusion.1
  525.7 1.7 fusion.69
  527.3 94.2 %reduce-scatter.8.cloned.1.call-done = f32[96,512]{1,0:T(8,128)} async-done(((f32[3072,512]{1,0:T(8,128)}), f32[96,512]{1,0:T(8,128)}) %reduce-scatter.8.cloned.1.call-update) | async-done | bytes 196624 | tf_op jit(solution)/shard_map/reduce_scatter | solution.py:109
  622.9 1.7 fusion.67
  624.6 1.7 fusion.64
  626.3 1.7 fusion.39
  628.0 1.8 fusion.41
  630.7 274.4 %all-reduce.3.cloned.1.call-done = (f32[512,512]{1,0:T(8,128)}, f32[512,512]{1,0:T(8,128)}, f32[512,512]{1,0:T(8,128)}, f32[512,512]{1,0:T(8,128)}, f32[512,512]{1,0:T(8,128)}) async-done(((f32[512,512]{1,0:T(8,128)}, f32[512,512]{1,0:T(8,128)}, f32[512,512]{1,0:T(8,128)}, f32[512,512]{1,0:T(8,128)}, f32[512,512]{1,0:T(8,128)}), (f32[512,512]{1,0:T(8,128)}, f32[512,512]{1,0:T(8,128)}, f32[512,512]{1,0:T(8,128)}, ...) | async-done | bytes 5242896 | tf_op jit(solution)/shard_map/psum | solution.py:76
  905.1 1.9 fusion.29
  907.6 2.6 fusion.13
  913.5 1.5 pad_maximum_fusion.1
  915.1 2.0 pad_maximum_fusion
  (64 shorter events, 14.2 us)
Async XLA Ops:
  7.2 159.4 %copy-start.8 = (s32[3,64]{1,0:T(4,128)S(1)}, s32[3,64]{1,0:T(4,128)}, u32[]{:S(2)}) copy-start(s32[3,64]{1,0:T(4,128)} %param.7) | copy-start | bytes 2308
  7.2 55.1 %all-gather.16.cloned.1.call-start = ((), (), s32[]{:S(2)}) async-start(), calls=%async_computation.6 | async-start | bytes 2162688 | tf_op jit(solution)/shard_map/all_gather | solution.py:84
  8.8 104.6 %all-gather.18.cloned.1.call-start = ((), (), s32[]{:S(2)}) async-start(), calls=%async_computation.7 | async-start | bytes 2162688 | tf_op jit(solution)/shard_map/all_gather | solution.py:84
  9.6 154.9 %all-gather.20.cloned.1.call-start = ((), (), s32[]{:S(2)}) async-start(), calls=%async_computation.8 | async-start | bytes 2162688 | tf_op jit(solution)/shard_map/all_gather | solution.py:84
  10.3 210.4 %all-gather.22.cloned.1.call-start = ((), (), s32[]{:S(2)}) async-start(), calls=%async_computation.9 | async-start | bytes 4718592 | tf_op jit(solution)/shard_map/all_gather | solution.py:13
  64.2 211.5 %all-gather.24.cloned.1.call-start = ((), (), s32[]{:S(2)}) async-start(), calls=%async_computation.10 | async-start | bytes 4718592 | tf_op jit(solution)/shard_map/all_gather | solution.py:13
  115.4 215.4 %all-gather.26.cloned.1.call-start = ((), (), s32[]{:S(2)}) async-start(), calls=%async_computation.11 | async-start | bytes 4718592 | tf_op jit(solution)/shard_map/all_gather | solution.py:13
  166.5 260.5 %reduce-scatter.4.cloned.1.call-start = ((), (), s32[]{:S(2)}) async-start(), calls=%async_computation.3 | async-start | bytes 6488064 | tf_op jit(solution)/shard_map/reduce_scatter | solution.py:109
  231.0 293.3 %reduce-scatter.6.cloned.1.call-start = ((), (), s32[]{:S(2)}) async-start(), calls=%async_computation.4 | async-start | bytes 6488064 | tf_op jit(solution)/shard_map/reduce_scatter | solution.py:109
  286.0 335.6 %reduce-scatter.8.cloned.1.call-start = ((), (), s32[]{:S(2)}) async-start(), calls=%async_computation.5 | async-start | bytes 6488064 | tf_op jit(solution)/shard_map/reduce_scatter | solution.py:109
  340.0 184.2 %copy-start = (bf16[2,512,512]{2,1,0:T(8,128)(2,1)S(1)}, bf16[2,512,512]{2,1,0:T(8,128)(2,1)}, u32[]{:S(2)}) copy-start(bf16[2,512,512]{2,1,0:T(8,128)(2,1)} %param.8) | copy-start | bytes 3145732
  340.0 565.1 %all-reduce.3.cloned.1.call-start = ((), (), s32[]{:S(2)}) async-start(), calls=%async_computation.12 | async-start | bytes 10485760 | tf_op jit(solution)/shard_map/psum | solution.py:76
  525.7 100.7 %copy-start.2 = (f32[96,512]{1,0:T(8,128)S(1)}, f32[96,512]{1,0:T(8,128)}, u32[]{:S(2)}) copy-start(f32[96,512]{1,0:T(8,128)} %reduce-scatter.4.cloned.1.call-done) | copy-start | bytes 589828
  622.8 5.1 copy-start.4
  622.9 5.1 copy-start.5
  905.1 2.5 copy-start.1
  907.0 3.2 copy-start.7
  910.2 1.2 copy-start.3
  910.2 2.2 copy-start.6
Sparse Core Ops, SparseCore 0:
  11.1 51.0 all-gather.15
  65.4 47.9 all-gather.17
  116.5 47.9 all-gather.19
  166.2 54.4 all-gather.21
  222.3 53.3 all-gather.23
  277.4 53.3 all-gather.25
  334.8 92.1 reduce-scatter.3
  431.0 93.2 reduce-scatter.5
  528.3 93.2 reduce-scatter.7
  630.0 275.0 all-reduce.2
